TPU v7x, 32 devices: a whole 2x2x4 slice. The times are simulated.
32 devices in a mesh: dp: 8 (over z, y), shard: 4 (over x, core).
Axes of the slice: x: 2, y: 2, z: 4, core: 2. Of those that a mesh axis runs over, the one named last changes fastest.
Arguments:
- tokens: bfloat16 [13312, 4096], P(('dp', 'shard')), may hold values from -6 to 6
- cotangent: bfloat16 [13312, 4096], P(('dp', 'shard')), may hold values from -6 to 6
- gate_up: bfloat16 [4, 4096, 256], P('shard'), may hold values from -0.09375 to 0.09375
- down: bfloat16 [4, 128, 4096], P('shard'), may hold values from -0.09375 to 0.09375
- kept_slots: int32 [2], replicated, may hold values from 0 to 3, as said below
Outputs:
- token_grad: bfloat16 [13312, 4096], P(('dp', 'shard'))
- grad_gate_up: bfloat16 [4, 4096, 256], P('shard', 'dp')
- grad_down: bfloat16 [4, 128, 4096], P('shard', None, 'dp')
Inputs may be any that keep to these rules, and one draw needn't show every extreme that they name: `kept_slots`: 2 distinct positions; position p is stored on index p // 1 of shard.
All inputs are finite; a program needn't handle non-finite values.
Results may differ from a plain program's by a relative error of at most 0.015.
Values may be sent and summed in bfloat16 or wider, within the bound.
A program may use at most 128 MiB of HBM per device.

v0:
```python
import math
import jax
import jax.numpy as jnp
from jax import lax
from jax.sharding import PartitionSpec as P


def spread(block, axis, source):
    block = jnp.where(lax.axis_index(axis) == source, block, jnp.zeros_like(block))
    return lax.psum(block, axis)


def body(tokens, cotangent, gate_up, down, kept_slots):
    slot_count = gate_up.shape[0]
    block_cols = down.shape[1]
    kept_count = kept_slots.shape[0]
    total_tokens = tokens.shape[0] * lax.axis_size("dp") * lax.axis_size("shard")
    scale_factor = 1.0 / math.sqrt(total_tokens)
    dx_total = jnp.zeros(tokens.shape, jnp.float32)
    pair_terms = []
    back_terms = []
    for kept_pos in range(kept_count):
        slot_id = kept_slots[kept_pos]
        local_slot = slot_id % slot_count
        owner_id = slot_id // slot_count
        own_pair = lax.dynamic_index_in_dim(gate_up, local_slot, 0, keepdims=False)
        own_back = lax.dynamic_index_in_dim(down, local_slot, 0, keepdims=False)
        w_pair, w_back = (spread(own_pair, "shard", owner_id), spread(own_back, "shard", owner_id))
        projected = jnp.dot(tokens, w_pair, preferred_element_type=jnp.float32)
        gate_pre = projected[:, :block_cols]
        up_pre = projected[:, block_cols:]
        sigmoid_gate = jax.nn.sigmoid(gate_pre)
        silu_gate = gate_pre * sigmoid_gate
        activated = (silu_gate * up_pre).astype(jnp.bfloat16)
        d_act = lax.dot_general(
            cotangent, w_back, (((1,), (1,)), ((), ())), preferred_element_type=jnp.float32
        )
        d_gate = d_act * up_pre * sigmoid_gate * (1.0 + gate_pre * (1.0 - sigmoid_gate))
        d_up = d_act * silu_gate
        d_projected = jnp.concatenate([d_gate, d_up], axis=1).astype(jnp.bfloat16)
        dx_total = dx_total + lax.dot_general(
            d_projected, w_pair, (((1,), (1,)), ((), ())), preferred_element_type=jnp.float32
        )
        pair_terms.append(
            lax.dot_general(
                tokens, d_projected, (((0,), (0,)), ((), ())), preferred_element_type=jnp.float32
            )
        )
        back_terms.append(
            lax.dot_general(
                activated, cotangent, (((0,), (0,)), ((), ())), preferred_element_type=jnp.float32
            )
        )
    pair_stack = jnp.stack(pair_terms)
    back_stack = jnp.stack(back_terms)
    pair_part, back_part = (
        lax.psum_scatter(
            pair_stack.astype(jnp.bfloat16), "dp", scatter_dimension=1, tiled=True
        ).astype(jnp.float32),
        lax.psum_scatter(
            back_stack.astype(jnp.bfloat16), "dp", scatter_dimension=2, tiled=True
        ).astype(jnp.float32),
    )
    pair_whole, back_whole = (
        lax.psum(pair_part.astype(jnp.bfloat16), "shard").astype(jnp.float32),
        lax.psum(back_part.astype(jnp.bfloat16), "shard").astype(jnp.float32),
    )
    my_slots = lax.axis_index("shard") * slot_count + jnp.arange(slot_count, dtype=jnp.int32)
    picking = (my_slots[:, None] == kept_slots[None, :]).astype(jnp.float32)
    pair_owned = jnp.einsum("sk,kab->sab", picking, pair_whole, precision=lax.Precision.HIGHEST)
    back_owned = jnp.einsum("sk,kab->sab", picking, back_whole, precision=lax.Precision.HIGHEST)
    return (
        dx_total.astype(jnp.bfloat16),
        (pair_owned * scale_factor).astype(jnp.bfloat16),
        (back_owned * scale_factor).astype(jnp.bfloat16),
    )


def solution(mesh):
    in_specs = (
        P(("dp", "shard"), None),
        P(("dp", "shard"), None),
        P("shard", None, None),
        P("shard", None, None),
        P(),
    )
    out_specs = (P(("dp", "shard"), None), P("shard", "dp", None), P("shard", None, "dp"))
    return jax.shard_map(body, mesh=mesh, in_specs=in_specs, out_specs=out_specs, check_vma=False)
```

profile of v0, /device:TPU:0, one launch (start us, length us, event | category | flops | bytes accessed | tf_op | source)
XLA Modules:
  0.0 355.7 jit_solution(2671473297520610019)
XLA Ops:
  7.2 0.0 copy-start
  7.2 0.0 all-reduce.7.cloned.1.call-start
  7.2 1.4 fusion.21
  9.9 0.0 copy-start.4
  10.0 2.9 select_bitcast_fusion.2
  12.8 0.0 copy-done.4
  12.8 2.3 select_bitcast_fusion
  15.1 0.0 all-reduce.7.cloned.1.call-update
  15.1 0.0 reduce-scatter.5.cloned.1.call-start
  15.2 122.9 %all-reduce.7.cloned.1.call-done = (bf16[4096,256]{1,0:T(8,128)(2,1)}, bf16[128,4096]{1,0:T(8,128)(2,1)}, bf16[4096,256]{1,0:T(8,128)(2,1)}, bf16[128,4096]{1,0:T(8,128)(2,1)}) async-done(((bf16[4096,256]{1,0:T(8,128)(2,1)}, bf16[128,4096]{1,0:T(8,128)(2,1)}, bf16[4096,256]{1,0:T(8,128)(2,1)}, bf16[128,4096]{1,0:T(8,128)(2,1)}), (bf16[4096,256]{1,0:T(8,128)(2,1)}, bf16[128,4096]{1,0:T(8,128)(2,1)}, ...) | async-done | bytes 6291472 | tf_op jit(solution)/shard_map/psum | solution.py:10
  138.1 0.0 copy-done
  138.1 0.0 copy-start.3
  138.1 2.8 convolution_bitcast_fusion.1
  140.9 0.0 copy-start.8
  140.9 0.0 copy-done.3
  140.9 0.0 copy-start.1
  141.0 1.1 convolution_bitcast_fusion
  142.0 1.0 copy-done.1
  143.1 0.0 copy-start.10
  143.1 0.8 fusion.3
  143.8 0.0 copy-done.8
  143.9 0.8 fusion.2
  144.6 0.0 copy-done.10
  144.6 1.5 pad_maximum_fusion.1
  146.2 0.0 reduce-scatter.5.cloned.1.call-update
  146.2 0.0 reduce-scatter.3.cloned.1.call-start
  146.2 3.4 multiply_convert_fusion.3
  149.6 0.0 copy-start.5
  149.6 0.0 copy-start.2
  149.6 0.0 copy-start.9
  149.7 0.0 copy-start.12
  149.7 1.3 fusion.1
  150.9 0.0 copy-done.5
  151.0 0.7 copy-done.2
  151.6 0.1 copy-done.9
  151.7 0.3 copy-done.12
  152.0 1.1 multiply_convert_fusion.5
  153.1 0.0 copy-start.6
  153.1 0.0 copy-start.7
  153.1 0.6 copy-done.6
  153.8 0.0 copy-done.7
  153.8 1.3 fusion
  155.1 2.4 pad_maximum_fusion
  157.5 0.0 copy-start.11
  157.5 0.0 reduce-scatter.3.cloned.1.call-update
  157.5 0.2 all-reduce.5.cloned.1.call-start
  157.8 0.4 copy-done.11
  158.2 5.7 %fusion.11 = f32[416,4096]{1,0:T(8,128)} fusion(bf16[4096,256]{1,0:T(8,128)(2,1)} %get-tuple-element.5, bf16[416,128]{1,0:T(8,128)(2,1)} %copy-done.7, bf16[416,128]{1,0:T(8,128)(2,1)} %copy-done.6), kind=kOutput, calls=%fused_computation.38 | convolution fusion | flops 872841216 | bytes 9125888 | tf_op jit(solution)/shard_map/dot_general | solution.py:41
  163.8 50.8 %reduce-scatter.5.cloned.1.call-done = bf16[2,128,512]{2,1,0:T(8,128)(2,1)} async-done(((bf16[2,128,4096]{2,1,0:T(8,128)(2,1)}), bf16[2,128,512]{2,1,0:T(8,128)(2,1)}) %reduce-scatter.5.cloned.1.call-update) | async-done | bytes 262160 | tf_op jit(solution)/shard_map/reduce_scatter | solution.py:60
  214.7 91.0 %reduce-scatter.3.cloned.1.call-done = bf16[2,512,256]{1,2,0:T(8,128)(2,1)} async-done(((bf16[2,4096,256]{1,2,0:T(8,128)(2,1)}), bf16[2,512,256]{1,2,0:T(8,128)(2,1)}) %reduce-scatter.3.cloned.1.call-update) | async-done | bytes 524304 | tf_op jit(solution)/shard_map/reduce_scatter | solution.py:57
  305.6 0.0 all-reduce.5.cloned.1.call-update
  305.7 6.4 %add_convert_fusion = bf16[416,4096]{1,0:T(8,128)(2,1)} fusion(f32[416,4096]{1,0:T(8,128)} %fusion.11, bf16[4096,256]{1,0:T(8,128)(2,1)} %get-tuple-element.7, bf16[416,128]{1,0:T(8,128)(2,1)} %copy-done.5, bf16[416,128]{1,0:T(8,128)(2,1)S(1)} %get-tuple-element.13), kind=kOutput, calls=%fused_computation | convolution fusion | flops 876249088 | bytes 12533760 | tf_op jit(solution)/shard_map/dot_general | solution.py:41
  312.1 30.5 %all-reduce.5.cloned.1.call-done = (bf16[2,512,256]{1,2,0:T(8,128)(2,1)}, bf16[2,128,512]{2,1,0:T(8,128)(2,1)}) async-done(((bf16[2,512,256]{1,2,0:T(8,128)(2,1)}, bf16[2,128,512]{2,1,0:T(8,128)(2,1)}), (bf16[2,512,256]{1,2,0:T(8,128)(2,1)}, bf16[2,128,512]{2,1,0:T(8,128)(2,1)})) %all-reduce.5.cloned.1.call-update) | async-done | bytes 786448 | tf_op jit(solution)/shard_map/psum | solution.py:65
  342.6 2.0 copy.8
  344.6 1.7 fusion.22
  346.3 0.8 fusion.5
  347.1 1.4 fusion.7
  348.4 0.7 fusion.12
  (1 shorter events, 0.0 us)
Async XLA Ops:
  7.2 131.0 %copy-start = (bf16[416,4096]{1,0:T(8,128)(2,1)S(1)}, bf16[416,4096]{1,0:T(8,128)(2,1)}, u32[]{:S(2)}) copy-start(bf16[416,4096]{1,0:T(8,128)(2,1)} %param.5) | copy-start | bytes 10223620
  7.2 130.9 %all-reduce.7.cloned.1.call-start = ((), (), s32[]{:S(2)}) async-start(), calls=%async_computation.5 | async-start | bytes 12582912 | tf_op jit(solution)/shard_map/psum | solution.py:10
  9.9 2.9 copy-start.4
  15.1 199.5 %reduce-scatter.5.cloned.1.call-start = ((), (), s32[]{:S(2)}) async-start(), calls=%async_computation.3 | async-start | bytes 2359296 | tf_op jit(solution)/shard_map/reduce_scatter | solution.py:60
  138.1 2.8 copy-start.3
  140.9 2.9 copy-start.8
  140.9 2.1 copy-start.1
  143.1 1.6 copy-start.10
  146.2 159.5 %reduce-scatter.3.cloned.1.call-start = ((), (), s32[]{:S(2)}) async-start(), calls=%async_computation.2 | async-start | bytes 4718592 | tf_op jit(solution)/shard_map/reduce_scatter | solution.py:57
  149.6 1.3 copy-start.5
  149.6 2.0 copy-start.2
  149.6 2.1 copy-start.9
  149.7 2.4 copy-start.12
  153.1 0.6 copy-start.6
  153.1 0.7 copy-start.7
  157.5 0.7 copy-start.11
  157.5 185.1 %all-reduce.5.cloned.1.call-start = ((), (), s32[]{:S(2)}) async-start(), calls=%async_computation.4 | async-start | bytes 1572864 | tf_op jit(solution)/shard_map/psum | solution.py:65
Sparse Core Ops, SparseCore 0:
  15.2 122.8 all-reduce.6
  146.3 68.3 reduce-scatter.4
  218.3 87.3 reduce-scatter.2
  308.1 34.3 all-reduce.4
where the time goes:
time: 356 us
  waiting for transfers between devices  295 us (83%)
  matrix products  27.6 us (8%)
  between operations  15.2 us (4%)
  other arithmetic  10.5 us (3%)
  local copies, waits for them, and re-layouts  6.64 us (2%)
    psum x1, waiting for transfers between devices, spread(): return lax.psum(block, axis)  123 us
    reduce_scatter x1, waiting for transfers between devices, body(): lax.psum_scatter(pair_stack.astype(jnp.bfloat16), 'dp', scatter_dimension...  91 us
    reduce_scatter x1, waiting for transfers between devices, body(): lax.psum_scatter(back_stack.astype(jnp.bfloat16), 'dp', scatter_dimension...  50.8 us
    psum x1, waiting for transfers between devices, body(): lax.psum(pair_part.astype(jnp.bfloat16), 'shard').astype(jnp.float32)  30.5 us
    dot_general x2, matrix products, body(): lax.dot_general(d_projected, w_pair, (((1,), (1,)), ((), ())), preferred_...  12.1 us
  transfers between devices with their start and end apart: 4, of which 4 were waited for; matrix products, arithmetic and copies ran while one was open for 6% of the time, Pallas kernels for 0%

commit v1 on v0

--- a/solution.py
+++ b/solution.py
@@ -3,6 +3,7 @@
 import jax.numpy as jnp
 from jax import lax
 from jax.sharding import PartitionSpec as P
+from jax.lax import all_gather
 
 
 def spread(block, axis, source):
@@ -62,7 +63,7 @@
         ).astype(jnp.float32),
     )
     pair_whole, back_whole = (
-        lax.psum(pair_part.astype(jnp.bfloat16), "shard").astype(jnp.float32),
+        jnp.sum(all_gather(pair_part.astype(jnp.bfloat16), "shard"), axis=0).astype(jnp.float32),
         lax.psum(back_part.astype(jnp.bfloat16), "shard").astype(jnp.float32),
     )
     my_slots = lax.axis_index("shard") * slot_count + jnp.arange(slot_count, dtype=jnp.int32)

time: 356 us -> 372 us (1.045)
  waiting for transfers between devices: 295 us -> 315 us
  matrix products: 27.6 us -> 21.4 us
  other arithmetic: 10.5 us -> 14.6 us
    psum x1 -> x0, waiting for transfers between devices: 30.5 us -> none  [body(): lax.psum(pair_part.astype(jnp.bfloat16), 'shard').astype(jnp.float32)]
    psum x1 -> x2, waiting for transfers between devices: 123 us -> 146 us  [spread(): return lax.psum(block, axis)]
    reduce_scatter x1, waiting for transfers between devices: 50.8 us -> 65.8 us  [body(): lax.psum_scatter(back_stack.astype(jnp.bfloat16), 'dp', scatter_dimension...]
    all_gather x0 -> x1, waiting for transfers between devices: none -> 14.6 us  [body(): all_gather(pair_part.astype(jnp.bfloat16), 'shard')]
    dot_general x2, matrix products: 12.1 us -> 5.79 us  [body(): lax.dot_general(d_projected, w_pair, (((1,), (1,)), ((), ())), preferred_...]
  transfers between devices with their start and end apart: 4 -> 5, of which waited for: 4 -> 5; matrix products, arithmetic and copies ran while one was open for 6% -> 3% of each run, Pallas kernels for 0% -> 0%
where the time goes in v1:
time: 372 us
  waiting for transfers between devices  315 us (85%)
  matrix products  21.4 us (6%)
  between operations  15.3 us (4%)
  other arithmetic  14.6 us (4%)
  local copies, waits for them, and re-layouts  4.79 us (1%)
    psum x2, waiting for transfers between devices, spread(): return lax.psum(block, axis)  146 us
    reduce_scatter x1, waiting for transfers between devices, body(): lax.psum_scatter(pair_stack.astype(jnp.bfloat16), 'dp', scatter_dimension...  88.2 us
    reduce_scatter x1, waiting for transfers between devices, body(): lax.psum_scatter(back_stack.astype(jnp.bfloat16), 'dp', scatter_dimension...  65.8 us
    all_gather x1, waiting for transfers between devices, body(): all_gather(pair_part.astype(jnp.bfloat16), 'shard')  14.6 us
  transfers between devices with their start and end apart: 5, of which 5 were waited for; matrix products, arithmetic and copies ran while one was open for 3% of the time, Pallas kernels for 0%

profile of v1, /device:TPU:0, one launch (start us, length us, event | category | flops | bytes accessed | tf_op | source)
XLA Modules:
  0.0 371.6 jit_solution(14715146809960354296)
XLA Ops:
  7.2 0.0 copy-start
  7.2 0.0 all-reduce.7.cloned.1.call-start
  7.2 1.4 fusion.23
  9.9 3.9 %select_bitcast_fusion = (bf16[4096,256]{1,0:T(8,128)(2,1)}, bf16[4096,256]{1,0:T(8,128)(2,1)}) fusion(bf16[1,4096,256]{2,1,0:T(8,128)(2,1)} %param.7, pred[]{:T(512)S(6)} %eq.21, pred[]{:T(512)S(6)} %eq.20), kind=kLoop, calls=%fused_computation.11 | loop fusion | flops 2097152 | bytes 6291458 | tf_op jit(solution)/shard_map/jit(_where)/select_n | solution.py:10
  13.8 0.0 all-reduce.7.cloned.1.call-update
  13.8 0.0 reduce-scatter.5.cloned.1.call-start
  13.9 88.5 %all-reduce.7.cloned.1.call-done = (bf16[4096,256]{1,0:T(8,128)(2,1)}, bf16[4096,256]{1,0:T(8,128)(2,1)}) async-done(((bf16[4096,256]{1,0:T(8,128)(2,1)}, bf16[4096,256]{1,0:T(8,128)(2,1)}), (bf16[4096,256]{1,0:T(8,128)(2,1)}, bf16[4096,256]{1,0:T(8,128)(2,1)})) %all-reduce.7.cloned.1.call-update) | async-done | bytes 4194320 | tf_op jit(solution)/shard_map/psum | solution.py:11
  102.4 0.0 copy-done
  102.4 0.0 copy-start.3
  102.4 2.8 convolution_bitcast_fusion.1
  105.2 0.0 copy-start.11
  105.2 0.0 copy-done.3
  105.2 0.0 copy-start.1
  105.2 1.1 convolution_bitcast_fusion
  106.3 1.0 copy-done.1
  107.3 0.0 copy-start.9
  107.3 0.8 fusion.3
  108.1 0.0 copy-done.11
  108.1 0.8 fusion.2
  108.9 0.0 copy-done.9
  108.9 1.5 pad_maximum_fusion.1
  110.4 0.0 reduce-scatter.5.cloned.1.call-update
  110.4 0.0 all-reduce.5.cloned.1.call-start
  110.5 2.7 select_bitcast_fusion.2
  113.1 65.8 %reduce-scatter.5.cloned.1.call-done = bf16[2,128,512]{2,1,0:T(8,128)(2,1)} async-done(((bf16[2,128,4096]{2,1,0:T(8,128)(2,1)}), bf16[2,128,512]{2,1,0:T(8,128)(2,1)}) %reduce-scatter.5.cloned.1.call-update) | async-done | bytes 262160 | tf_op jit(solution)/shard_map/reduce_scatter | solution.py:61
  179.0 0.0 all-reduce.5.cloned.1.call-update
  179.0 0.0 reduce-scatter.3.cloned.1.call-start
  179.0 57.8 %all-reduce.5.cloned.1.call-done = (bf16[128,4096]{1,0:T(8,128)(2,1)}, bf16[128,4096]{1,0:T(8,128)(2,1)}, bf16[2,128,512]{2,1,0:T(8,128)(2,1)}) async-done(((bf16[128,4096]{1,0:T(8,128)(2,1)}, bf16[128,4096]{1,0:T(8,128)(2,1)}, bf16[2,128,512]{2,1,0:T(8,128)(2,1)}), (bf16[128,4096]{1,0:T(8,128)(2,1)}, bf16[128,4096]{1,0:T(8,128)(2,1)}, bf16[2,128,512]{2,1,0:T(8,128)(2,1)})) %all-reduce.5.cloned.1.call-update) | async-done | bytes 2359312 | tf_op jit(solution)/shard_map/psum | solution.py:11
  236.8 0.0 copy-start.2
  236.8 0.0 copy-start.10
  236.8 0.0 copy-start.13
  236.8 3.5 multiply_convert_fusion.5
  240.4 0.0 copy-start.7
  240.4 0.0 copy-start.8
  240.4 0.0 copy-done.2
  240.4 0.0 copy-done.10
  240.4 0.2 copy-done.13
  240.7 1.1 multiply_convert_fusion.3
  241.7 0.0 copy-start.5
  241.8 1.3 fusion.1
  243.0 0.0 copy-done.5
  243.0 0.0 copy-done.7
  243.1 0.0 copy-done.8
  243.1 1.3 fusion
  244.3 2.3 pad_maximum_fusion
  246.6 0.0 copy-start.12
  246.6 0.0 reduce-scatter.3.cloned.1.call-update
  246.7 0.2 all-gather.3.cloned.1.call-start
  246.9 88.2 %reduce-scatter.3.cloned.1.call-done = bf16[2,512,256]{1,2,0:T(8,128)(2,1)} async-done(((bf16[2,4096,256]{1,2,0:T(8,128)(2,1)}), bf16[2,512,256]{1,2,0:T(8,128)(2,1)}) %reduce-scatter.3.cloned.1.call-update) | async-done | bytes 524304 | tf_op jit(solution)/shard_map/reduce_scatter | solution.py:58
  335.2 2.0 copy.8
  337.2 0.0 all-gather.3.cloned.1.call-update
  337.2 0.0 copy-done.12
  337.2 1.4 fusion.9
  338.6 0.7 fusion.14
  339.3 0.0 copy-start.4
  339.3 0.0 copy-start.6
  339.3 2.9 fusion.13
  342.2 0.0 copy-done.4
  342.2 0.0 copy-done.6
  342.2 2.9 add_convert_fusion
  345.1 14.6 %all-gather.3.cloned.1.call-done = bf16[8,512,256]{2,1,0:T(8,128)(2,1)} async-done(((bf16[2,512,256]{2,1,0:T(8,128)(2,1)}), bf16[8,512,256]{2,1,0:T(8,128)(2,1)}) %all-gather.3.cloned.1.call-update) | async-done | bytes 2097168 | tf_op jit(solution)/shard_map/all_gather | solution.py:66
  359.7 2.8 reduce_sum.12
  362.5 1.7 fusion.5
  364.3 0.8 fusion.7
Async XLA Ops:
  7.2 95.2 %copy-start = (bf16[416,4096]{1,0:T(8,128)(2,1)S(1)}, bf16[416,4096]{1,0:T(8,128)(2,1)}, u32[]{:S(2)}) copy-start(bf16[416,4096]{1,0:T(8,128)(2,1)} %param.5) | copy-start | bytes 10223620
  7.2 95.2 %all-reduce.7.cloned.1.call-start = ((), (), s32[]{:S(2)}) async-start(), calls=%async_computation.6 | async-start | bytes 8388608 | tf_op jit(solution)/shard_map/psum | solution.py:11
  13.8 165.1 %reduce-scatter.5.cloned.1.call-start = ((), (), s32[]{:S(2)}) async-start(), calls=%async_computation.3 | async-start | bytes 2359296 | tf_op jit(solution)/shard_map/reduce_scatter | solution.py:61
  102.4 2.8 copy-start.3
  105.2 2.9 copy-start.11
  105.2 2.1 copy-start.1
  107.3 1.6 copy-start.9
  110.4 126.4 %all-reduce.5.cloned.1.call-start = ((), (), s32[]{:S(2)}) async-start(), calls=%async_computation.5 | async-start | bytes 4718592 | tf_op jit(solution)/shard_map/psum | solution.py:11
  179.0 156.2 %reduce-scatter.3.cloned.1.call-start = ((), (), s32[]{:S(2)}) async-start(), calls=%async_computation.2 | async-start | bytes 4718592 | tf_op jit(solution)/shard_map/reduce_scatter | solution.py:58
  236.8 3.6 copy-start.2
  236.8 3.6 copy-start.10
  236.8 3.8 %copy-start.13 = (bf16[128,4096]{1,0:T(8,128)(2,1)S(1)}, bf16[128,4096]{1,0:T(8,128)(2,1)}, u32[]{:S(2)}) copy-start(bf16[128,4096]{1,0:T(8,128)(2,1)} %get-tuple-element.4) | copy-start | bytes 3145732
  240.4 2.7 copy-start.7
  240.4 2.7 copy-start.8
  241.7 1.3 copy-start.5
  246.6 90.6 %copy-start.12 = (s32[2]{0:T(128)S(1)}, s32[2]{0:T(128)}, u32[]{:S(2)}) copy-start(s32[2]{0:T(128)} %param.9) | copy-start | bytes 28
  246.7 113.0 %all-gather.3.cloned.1.call-start = ((), (), s32[]{:S(2)}) async-start(), calls=%async_computation.4 | async-start | bytes 2621440 | tf_op jit(solution)/shard_map/all_gather | solution.py:66
  339.3 2.9 copy-start.4
  339.3 2.9 copy-start.6
Sparse Core Ops, SparseCore 0:
  14.0 88.3 all-reduce.6
  110.5 68.3 reduce-scatter.4
  181.7 55.1 all-reduce.4
  246.8 88.3 reduce-scatter.2
  337.3 22.3 all-gather.2
